TPU v7x, 256 devices: a whole 4x4x8 slice. The times are simulated.
256 devices in a mesh: row: 16 (over x_hi, y, core), col: 16 (over z, x_lo).
Axes of the slice: x: 4 (x_hi: 2, x_lo: 2; x = x_hi * 2 + x_lo), y: 4, z: 8, core: 2. Of those that a mesh axis runs over, the one named last changes fastest.
Arguments:
- vectors: float32 [96, 65536], P(None, ('col', 'row')), may hold values from -6 to 6
- blocks: float32 [16, 16, 176, 128, 128], P('row', 'col'), may hold values from -0.0546875 to 0.0546875
- block_row: int32 [16, 16, 176], P('row', 'col'), may hold values from 0 to 31
- block_col: int32 [16, 16, 176], P('row', 'col'), may hold values from 0 to 31
- block_count: int32 [16, 16], P('row', 'col'), may hold values from 22 to 176, as said below
- lower_bound: float32 [1], replicated, may hold values from -2.5 to -1.5
- upper_bound: float32 [1], replicated, may hold values from 1.5 to 2.5
Outputs:
- filtered: float32 [96, 65536], P(None, ('col', 'row'))
Inputs may be any that keep to these rules, and one draw needn't show every extreme that they name: `block_row`: local block row index within the device's band. `block_col`: local block column index within the device's band. `block_count`: in every row of the device grid one device has all 176 slots stored.
All inputs are finite; a program needn't handle non-finite values.
Results may differ from a plain program's by a relative error of at most 0.0003.
Values sent between devices are 32-bit elements; how exact they have to be, the bound alone decides.
No kernel may reach another device: no remote copies, remote signals or barrier semaphores. Data moves between devices by JAX's collectives and lax.ppermute only.
A program may use at most 128 MiB of HBM per device.

v0:
```python
import jax
import jax.numpy as jnp
from jax import lax
from jax.sharding import PartitionSpec as P

BS = 128


def spread(value, axis, source):
    kept = jnp.where(lax.axis_index(axis) == source, value, 0).astype(value.dtype)
    return lax.psum(kept, axis)


def local_products(col_tile, row_tile, device_blocks, rows_local, cols_local, live_mask):
    vector_count = col_tile.shape[0]
    col_blocks = col_tile.shape[1] // BS
    row_blocks = row_tile.shape[1] // BS
    col_view = col_tile.reshape(vector_count, col_blocks, BS)
    row_view = row_tile.reshape(vector_count, row_blocks, BS)
    source_col = jnp.take(col_view, cols_local, axis=1)
    forward = jnp.einsum("sij,vsj->vsi", device_blocks, source_col, precision=lax.Precision.HIGHEST)
    source_row = jnp.take(row_view, rows_local, axis=1)
    backward = jnp.einsum(
        "sij,vsi->vsj", device_blocks, source_row, precision=lax.Precision.HIGHEST
    )
    row_onehot = (jnp.arange(row_blocks)[:, None] == rows_local[None, :]).astype(
        jnp.float32
    ) * live_mask[None, :]
    col_onehot = (jnp.arange(col_blocks)[:, None] == cols_local[None, :]).astype(
        jnp.float32
    ) * live_mask[None, :]
    forward_part = jnp.einsum("rs,vsi->vri", row_onehot, forward, precision=lax.Precision.HIGHEST)
    backward_part = jnp.einsum("cs,vsj->vcj", col_onehot, backward, precision=lax.Precision.HIGHEST)
    return (forward_part.reshape(vector_count, -1), backward_part.reshape(vector_count, -1))


def apply_hamiltonian(vectors, device_blocks, rows_local, cols_local, live_mask):
    col_tile = lax.all_gather(vectors, "row", axis=1, tiled=True)
    row_index = lax.axis_index("row")
    col_index = lax.axis_index("col")
    col_count = lax.axis_size("col")
    row_ratio = lax.axis_size("row") // col_count
    piece_size = vectors.shape[1]
    owner_flag = (row_index // row_ratio == col_index).astype(jnp.float32)
    row_tile = spread(col_tile, "col", row_index // row_ratio)
    forward_part, backward_part = local_products(
        col_tile, row_tile, device_blocks, rows_local, cols_local, live_mask
    )
    row_total = lax.psum(forward_part, "col")
    placed = row_total * owner_flag
    column_total = lax.psum(placed, "row")
    backward_sum = lax.psum_scatter(backward_part, "row", scatter_dimension=1, tiled=True)
    return backward_sum + lax.dynamic_slice_in_dim(
        column_total, row_index * piece_size, piece_size, 1
    )


def body(vectors, blocks, block_row, block_col, block_count, lower_bound, upper_bound):
    device_blocks = blocks[0, 0]
    rows_local = block_row[0, 0]
    cols_local = block_col[0, 0]
    live_mask = (jnp.arange(device_blocks.shape[0]) < block_count[0, 0]).astype(jnp.float32)
    center = (upper_bound[0] + lower_bound[0]) / 2.0
    half_width = (upper_bound[0] - lower_bound[0]) / 2.0
    previous = vectors
    product = apply_hamiltonian(vectors, device_blocks, rows_local, cols_local, live_mask)
    current = (product - center * vectors) / half_width
    product = apply_hamiltonian(current, device_blocks, rows_local, cols_local, live_mask)
    following = 2.0 * (product - center * current) / half_width - previous
    previous, current = (current, following)
    return current


def solution(mesh):
    placed = (
        P(None, ("col", "row")),
        P("row", "col", None, None, None),
        P("row", "col", None),
        P("row", "col", None),
        P("row", "col"),
        P(),
        P(),
    )
    return jax.shard_map(
        body, mesh=mesh, in_specs=placed, out_specs=P(None, ("col", "row")), check_vma=False
    )
```

profile of v0, /device:TPU:32, one launch (start us, length us, event | category | flops | bytes accessed | tf_op | source)
XLA Modules:
  0.0 1001.6 jit_solution(16163257239828997144)
XLA Ops:
  9.3 52.8 %all-gather.3.cloned.1.call-done = f32[96,4096]{1,0:T(8,128)} async-done(((f32[96,256]{1,0:T(8,128)}), f32[96,4096]{1,0:T(8,128)}) %all-gather.3.cloned.1.call-update) | async-done | bytes 1572880 | tf_op jit(solution)/shard_map/all_gather | solution.py:38
  62.1 1.6 copy_bitcast_fusion.6
  63.7 4.5 gather_fusion.1
  68.2 26.9 %fusion.37 = f32[96,176,128]{2,0,1:T(8,128)S(1)} fusion(f32[1,1,176,128,128]{4,3,2,1,0:T(8,128)} %param.10, f32[176,96,128]{2,1,0:T(8,128)} %gather_fusion.1, pred[176]{0:T(512)(128)(4,1)S(1)} %compare_and_fusion.1), kind=kOutput, calls=%fused_computation.37 | convolution fusion | flops 3324051456 | bytes 28836016 | tf_op jit(solution)/shard_map/sij,vsj->vsi/dot_general | solution.py:21
  95.1 9.6 fusion.16
  104.7 2.3 copy.42
  107.0 1.4 copy_bitcast_fusion.7
  108.5 160.6 %all-reduce.13.cloned.1.call-done = (f32[96,32,128]{2,0,1:T(8,128)}, f32[96,4096]{1,0:T(8,128)}) async-done(((f32[96,32,128]{2,0,1:T(8,128)}, f32[96,4096]{1,0:T(8,128)}), (f32[96,32,128]{2,0,1:T(8,128)}, f32[96,4096]{1,0:T(8,128)})) %all-reduce.13.cloned.1.call-update) | async-done | bytes 3145744 | tf_op jit(solution)/shard_map/psum | solution.py:11
  269.1 2.8 broadcast_multiply_fusion.1
  272.0 4.5 gather_fusion
  276.5 14.7 %fusion.32 = f32[96,176,128]{2,0,1:T(8,128)S(1)} fusion(f32[1,1,176,128,128]{4,3,2,1,0:T(8,128)} %param.10, f32[176,96,128]{2,1,0:T(8,128)} %gather_fusion, pred[176]{0:T(512)(128)(4,1)S(1)} %compare_and_fusion), kind=kOutput, calls=%fused_computation.36 | convolution fusion | flops 3324051456 | bytes 28836016 | tf_op jit(solution)/shard_map/sij,vsi->vsj/dot_general | solution.py:23
  291.2 9.6 fusion.18
  300.8 2.3 copy.43
  304.4 115.3 %all-reduce.7.cloned.1.call-done = f32[96,4096]{1,0:T(8,128)} async-done(((f32[96,4096]{1,0:T(8,128)}), f32[96,4096]{1,0:T(8,128)}) %all-reduce.7.cloned.1.call-update) | async-done | bytes 1572880 | tf_op jit(solution)/shard_map/psum | solution.py:51
  419.8 81.7 %reduce-scatter.3.cloned.1.call-done = f32[96,256]{1,0:T(8,128)} async-done(((f32[96,4096]{1,0:T(8,128)}), f32[96,256]{1,0:T(8,128)}) %reduce-scatter.3.cloned.1.call-update) | async-done | bytes 98320 | tf_op jit(solution)/shard_map/reduce_scatter | solution.py:52
  501.5 1.6 subtract_divide_fusion
  503.2 49.5 %all-gather.5.cloned.1.call-done = f32[96,4096]{1,0:T(8,128)} async-done(((f32[96,256]{1,0:T(8,128)}), f32[96,4096]{1,0:T(8,128)}) %all-gather.5.cloned.1.call-update) | async-done | bytes 1572880 | tf_op jit(solution)/shard_map/all_gather | solution.py:38
  552.6 1.6 copy_bitcast_fusion.4
  554.2 4.5 gather_fusion.3
  558.7 26.9 %fusion.47 = f32[96,176,128]{2,0,1:T(8,128)S(1)} fusion(f32[1,1,176,128,128]{4,3,2,1,0:T(8,128)} %param.10, f32[176,96,128]{2,1,0:T(8,128)} %gather_fusion.3, pred[176]{0:T(512)(128)(4,1)S(1)} %compare_and_fusion.1), kind=kOutput, calls=%fused_computation.39 | convolution fusion | flops 3324051456 | bytes 28836016 | tf_op jit(solution)/shard_map/sij,vsj->vsi/dot_general | solution.py:21
  585.6 9.6 fusion.12
  595.2 2.3 copy.40
  597.4 1.4 copy_bitcast_fusion.5
  598.9 161.4 %all-reduce.11.cloned.1.call-done = (f32[96,32,128]{2,0,1:T(8,128)}, f32[96,4096]{1,0:T(8,128)}) async-done(((f32[96,32,128]{2,0,1:T(8,128)}, f32[96,4096]{1,0:T(8,128)}), (f32[96,32,128]{2,0,1:T(8,128)}, f32[96,4096]{1,0:T(8,128)})) %all-reduce.11.cloned.1.call-update) | async-done | bytes 3145744 | tf_op jit(solution)/shard_map/psum | solution.py:11
  760.4 2.8 broadcast_multiply_fusion
  763.5 4.5 gather_fusion.2
  767.9 14.3 %fusion.42 = f32[96,176,128]{2,0,1:T(8,128)S(1)} fusion(f32[1,1,176,128,128]{4,3,2,1,0:T(8,128)} %param.10, f32[176,96,128]{2,1,0:T(8,128)} %gather_fusion.2, pred[176]{0:T(512)(128)(4,1)S(1)} %compare_and_fusion), kind=kOutput, calls=%fused_computation.38 | convolution fusion | flops 3324051456 | bytes 28836016 | tf_op jit(solution)/shard_map/sij,vsi->vsj/dot_general | solution.py:23
  782.3 9.6 fusion.14
  791.8 2.3 copy.41
  794.1 116.9 %all-reduce.9.cloned.1.call-done = f32[96,4096]{1,0:T(8,128)} async-done(((f32[96,4096]{1,0:T(8,128)}), f32[96,4096]{1,0:T(8,128)}) %all-reduce.9.cloned.1.call-update) | async-done | bytes 1572880 | tf_op jit(solution)/shard_map/psum | solution.py:51
  911.1 81.9 %reduce-scatter.5.cloned.1.call-done = f32[96,256]{1,0:T(8,128)} async-done(((f32[96,4096]{1,0:T(8,128)}), f32[96,256]{1,0:T(8,128)}) %reduce-scatter.5.cloned.1.call-update) | async-done | bytes 98320 | tf_op jit(solution)/shard_map/reduce_scatter | solution.py:52
  992.9 1.6 divide_subtract_fusion
  (39 shorter events, 2.8 us)
Async XLA Ops:
  6.5 55.6 %all-gather.3.cloned.1.call-start = ((), (), s32[]{:S(2)}) async-start(), calls=%async_computation.2 | async-start | bytes 1671168 | tf_op jit(solution)/shard_map/all_gather | solution.py:38
  7.3 261.8 %all-reduce.13.cloned.1.call-start = ((), (), s32[]{:S(2)}) async-start(), calls=%async_computation.9 | async-start | bytes 6291456 | tf_op jit(solution)/shard_map/psum | solution.py:11
  68.2 26.9 %copy-start.6 = (s32[1,1,176]{2,1,0:T(1,128)S(1)}, s32[1,1,176]{2,1,0:T(1,128)}, u32[]{:S(2)}) copy-start(s32[1,1,176]{2,1,0:T(1,128)} %param.11) | copy-start | bytes 2116
  95.1 11.9 %copy-start.2 = (f32[96,4096]{1,0:T(8,128)S(1)}, f32[96,4096]{1,0:T(8,128)}, u32[]{:S(2)}) copy-start(f32[96,4096]{1,0:T(8,128)} %all-gather.3.cloned.1.call-done) | copy-start | bytes 4718596
  108.4 311.4 %all-reduce.7.cloned.1.call-start = ((), (), s32[]{:S(2)}) async-start(), calls=%async_computation.4 | async-start | bytes 3145728 | tf_op jit(solution)/shard_map/psum | solution.py:51
  269.1 2.9 copy-start
  271.9 229.6 %reduce-scatter.3.cloned.1.call-start = ((), (), s32[]{:S(2)}) async-start(), calls=%async_computation.3 | async-start | bytes 1671168 | tf_op jit(solution)/shard_map/reduce_scatter | solution.py:52
  276.5 14.7 %copy-start.7 = (s32[1,1,176]{2,1,0:T(1,128)S(1)}, s32[1,1,176]{2,1,0:T(1,128)}, u32[]{:S(2)}) copy-start(s32[1,1,176]{2,1,0:T(1,128)} %param.12) | copy-start | bytes 2116
  291.2 210.3 %copy-start.4 = (f32[96,256]{1,0:T(8,128)S(1)}, f32[96,256]{1,0:T(8,128)}, u32[]{:S(2)}) copy-start(f32[96,256]{1,0:T(8,128)} %param.9) | copy-start | bytes 294916
  303.1 249.6 %all-gather.5.cloned.1.call-start = ((), (), s32[]{:S(2)}) async-start(), calls=%async_computation.5 | async-start | bytes 1671168 | tf_op jit(solution)/shard_map/all_gather | solution.py:38
  503.1 257.2 %all-reduce.11.cloned.1.call-start = ((), (), s32[]{:S(2)}) async-start(), calls=%async_computation.8 | async-start | bytes 6291456 | tf_op jit(solution)/shard_map/psum | solution.py:11
  585.6 11.8 %copy-start.3 = (f32[96,4096]{1,0:T(8,128)S(1)}, f32[96,4096]{1,0:T(8,128)}, u32[]{:S(2)}) copy-start(f32[96,4096]{1,0:T(8,128)} %all-gather.5.cloned.1.call-done) | copy-start | bytes 4718596
  598.9 312.2 %all-reduce.9.cloned.1.call-start = ((), (), s32[]{:S(2)}) async-start(), calls=%async_computation.7 | async-start | bytes 3145728 | tf_op jit(solution)/shard_map/psum | solution.py:51
  760.4 3.1 copy-start.1
  763.2 229.7 %reduce-scatter.5.cloned.1.call-start = ((), (), s32[]{:S(2)}) async-start(), calls=%async_computation.6 | async-start | bytes 1671168 | tf_op jit(solution)/shard_map/reduce_scatter | solution.py:52
  782.3 210.7 %copy-start.5 = (f32[96,256]{1,0:T(8,128)S(1)}, f32[96,256]{1,0:T(8,128)}, u32[]{:S(2)}) copy-start(f32[96,256]{1,0:T(8,128)} %subtract_divide_fusion) | copy-start | bytes 294916
Sparse Core Ops, SparseCore 0:
  9.9 52.1 all-gather.2
  108.5 160.5 all-reduce.12
  272.0 147.6 all-reduce.6
  423.8 77.6 reduce-scatter.2
  503.9 48.6 all-gather.4
  599.0 161.3 all-reduce.10
  763.3 147.6 all-reduce.8
  915.3 77.6 reduce-scatter.4
where the time goes:
time: 1010 us; the launch traced here: 1000 us
  waiting for transfers between devices  821 us (81%)
  matrix products  121 us (12%)
  local copies, waits for them, and re-layouts  30.1 us (3%)
  between operations  15.9 us (2%)
  other arithmetic  13 us (1%)
    psum x2, waiting for transfers between devices, spread(): return lax.psum(kept, axis)  322 us
    psum x2, waiting for transfers between devices, apply_hamiltonian(): column_total = lax.psum(placed, 'row')  232 us
    reduce_scatter x2, waiting for transfers between devices, apply_hamiltonian(): lax.psum_scatter(backward_part, 'row', scatter_dimension=1, tiled=True)  164 us
    all_gather x2, waiting for transfers between devices, apply_hamiltonian(): col_tile = lax.all_gather(vectors, 'row', axis=1, tiled=True)  102 us
    dot_general x2, matrix products, local_products(): jnp.einsum('sij,vsj->vsi', device_blocks, source_col, precision=lax.Preci...  53.8 us
    dot_general x2, matrix products, local_products(): jnp.einsum('sij,vsi->vsj', device_blocks, source_row, precision=lax.Preci...  29 us
  transfers between devices with their start and end apart: 8, of which 8 were waited for; matrix products, arithmetic and copies ran while one was open for 6% of the time, Pallas kernels for 0%

commit v1 on v0

--- a/solution.py
+++ b/solution.py
@@ -35,7 +35,9 @@
 
 
 def apply_hamiltonian(vectors, device_blocks, rows_local, cols_local, live_mask):
-    col_tile = lax.all_gather(vectors, "row", axis=1, tiled=True)
+    col_tile = jnp.concatenate(
+        jax.lax.all_to_all(jnp.stack(jax.lax.axis_size("row") * [vectors], 0), "row", 0, 0), 1
+    )
     row_index = lax.axis_index("row")
     col_index = lax.axis_index("col")
     col_count = lax.axis_size("col")

time: 1010 us -> 978 us (0.968)
  waiting for transfers between devices: 821 us -> 738 us
  blocking collectives: 0 us -> 28.2 us
  local copies, waits for them, and re-layouts: 30.1 us -> 49.6 us
    all_gather x2 -> x0, waiting for transfers between devices: 102 us -> none  [apply_hamiltonian(): col_tile = lax.all_gather(vectors, 'row', axis=1, tiled=True)]
    all_to_all x0 -> x1, blocking collectives: none -> 28.2 us  [apply_hamiltonian(): jax.lax.all_to_all(jnp.stack(jax.lax.axis_size('row') * [vectors], 0), 'r...]
    all_to_all x0 -> x1, waiting for transfers between devices: none -> 21.6 us  [apply_hamiltonian(): jax.lax.all_to_all(jnp.stack(jax.lax.axis_size('row') * [vectors], 0), 'r...]
  transfers between devices with their start and end apart: 8 -> 7, of which waited for: 8 -> 7; matrix products, arithmetic and copies ran while one was open for 6% -> 6% of each run, Pallas kernels for 0% -> 0%
where the time goes in v1:
time: 978 us; the launch traced here: 970 us
  waiting for transfers between devices  738 us (75%)
  matrix products  122 us (12%)
  local copies, waits for them, and re-layouts  49.6 us (5%)
  blocking collectives  28.2 us (3%)
  between operations  15.8 us (2%)
  other arithmetic  9.88 us (1%)
    psum x2, waiting for transfers between devices, spread(): return lax.psum(kept, axis)  320 us
    psum x2, waiting for transfers between devices, apply_hamiltonian(): column_total = lax.psum(placed, 'row')  233 us
    reduce_scatter x2, waiting for transfers between devices, apply_hamiltonian(): lax.psum_scatter(backward_part, 'row', scatter_dimension=1, tiled=True)  164 us
    dot_general x2, matrix products, local_products(): jnp.einsum('sij,vsj->vsi', device_blocks, source_col, precision=lax.Preci...  54.3 us
    dot_general x2, matrix products, local_products(): jnp.einsum('sij,vsi->vsj', device_blocks, source_row, precision=lax.Preci...  28.9 us
    all_to_all x1, blocking collectives, apply_hamiltonian(): jax.lax.all_to_all(jnp.stack(jax.lax.axis_size('row') * [vectors], 0), 'r...  28.2 us
    all_to_all x1, waiting for transfers between devices, apply_hamiltonian(): jax.lax.all_to_all(jnp.stack(jax.lax.axis_size('row') * [vectors], 0), 'r...  21.6 us
  transfers between devices with their start and end apart: 7, of which 7 were waited for; matrix products, arithmetic and copies ran while one was open for 6% of the time, Pallas kernels for 0%

profile of v1, /device:TPU:32, one launch (start us, length us, event | category | flops | bytes accessed | tf_op | source)
XLA Modules:
  0.0 970.4 jit_solution(8747368352828512050)
XLA Ops:
  6.5 2.2 stack.4
  8.7 7.0 all-to-all-start
  17.9 21.6 %all-to-all-done = f32[16,96,256]{2,1,0:T(8,128)S(1)} async-done(((f32[16,96,256]{2,1,0:T(8,128)}), f32[16,96,256]{2,1,0:T(8,128)S(1)}, u32[]{:S(2)}, u32[]{:S(2)}) %all-to-all-start) | async-done | bytes 1572896 | tf_op jit(solution)/shard_map/all_to_all | solution.py:39
  41.6 2.3 copy.20
  46.2 3.5 copy.17
  49.8 4.5 gather_fusion.1
  54.2 27.2 %fusion.37 = f32[96,176,128]{2,0,1:T(8,128)S(1)} fusion(f32[1,1,176,128,128]{4,3,2,1,0:T(8,128)} %param.10, f32[176,96,128]{2,1,0:T(8,128)} %gather_fusion.1, pred[176]{0:T(512)(128)(4,1)S(1)} %compare_and_fusion.1), kind=kOutput, calls=%fused_computation.37 | convolution fusion | flops 3324051456 | bytes 28836016 | tf_op jit(solution)/shard_map/sij,vsj->vsi/dot_general | solution.py:21
  81.5 9.6 fusion.16
  91.0 2.2 copy.46
  93.4 161.0 %all-reduce.13.cloned.1.call-done = (f32[96,32,128]{2,0,1:T(8,128)}, f32[96,4096]{1,0:T(8,128)}) async-done(((f32[96,32,128]{2,0,1:T(8,128)}, f32[96,4096]{1,0:T(8,128)}), (f32[96,32,128]{2,0,1:T(8,128)}, f32[96,4096]{1,0:T(8,128)})) %all-reduce.13.cloned.1.call-update) | async-done | bytes 3145744 | tf_op jit(solution)/shard_map/psum | solution.py:11
  254.4 2.8 broadcast_multiply_fusion.1
  257.3 4.5 gather_fusion
  261.8 14.5 %fusion.32 = f32[96,176,128]{2,0,1:T(8,128)S(1)} fusion(f32[1,1,176,128,128]{4,3,2,1,0:T(8,128)} %param.10, f32[176,96,128]{2,1,0:T(8,128)} %gather_fusion, pred[176]{0:T(512)(128)(4,1)S(1)} %compare_and_fusion), kind=kOutput, calls=%fused_computation.36 | convolution fusion | flops 3324051456 | bytes 28836016 | tf_op jit(solution)/shard_map/sij,vsi->vsj/dot_general | solution.py:23
  276.3 9.6 fusion.18
  285.8 2.3 copy.47
  289.5 115.6 %all-reduce.7.cloned.1.call-done = f32[96,4096]{1,0:T(8,128)} async-done(((f32[96,4096]{1,0:T(8,128)}), f32[96,4096]{1,0:T(8,128)}) %all-reduce.7.cloned.1.call-update) | async-done | bytes 1572880 | tf_op jit(solution)/shard_map/psum | solution.py:53
  405.1 81.9 %reduce-scatter.3.cloned.1.call-done = f32[96,256]{1,0:T(8,128)} async-done(((f32[96,4096]{1,0:T(8,128)}), f32[96,256]{1,0:T(8,128)}) %reduce-scatter.3.cloned.1.call-update) | async-done | bytes 98320 | tf_op jit(solution)/shard_map/reduce_scatter | solution.py:54
  488.1 28.2 %all_to_all.10 = f32[16,96,256]{2,1,0:T(8,128)S(1)} all-to-all(f32[16,96,256]{2,1,0:T(8,128)S(1)} %stack.5), channel_id=1, replica_groups=mesh['row'=16,'col'=16] {'row'}, dimensions={0} | all-to-all | bytes 3145728 | tf_op jit(solution)/shard_map/all_to_all | solution.py:39
  518.6 3.5 copy.23
  524.3 2.3 copy.26
  526.6 4.5 gather_fusion.3
  531.1 27.1 %fusion.47 = f32[96,176,128]{2,0,1:T(8,128)S(1)} fusion(f32[1,1,176,128,128]{4,3,2,1,0:T(8,128)} %param.10, f32[176,96,128]{2,1,0:T(8,128)} %gather_fusion.3, pred[176]{0:T(512)(128)(4,1)S(1)} %compare_and_fusion.1), kind=kOutput, calls=%fused_computation.39 | convolution fusion | flops 3324051456 | bytes 28836016 | tf_op jit(solution)/shard_map/sij,vsj->vsi/dot_general | solution.py:21
  558.2 9.6 fusion.12
  567.8 2.2 copy.44
  570.1 159.2 %all-reduce.11.cloned.1.call-done = (f32[96,32,128]{2,0,1:T(8,128)}, f32[96,4096]{1,0:T(8,128)}) async-done(((f32[96,32,128]{2,0,1:T(8,128)}, f32[96,4096]{1,0:T(8,128)}), (f32[96,32,128]{2,0,1:T(8,128)}, f32[96,4096]{1,0:T(8,128)})) %all-reduce.11.cloned.1.call-update) | async-done | bytes 3145744 | tf_op jit(solution)/shard_map/psum | solution.py:11
  729.3 2.8 broadcast_multiply_fusion
  732.2 4.5 gather_fusion.2
  736.7 14.5 %fusion.42 = f32[96,176,128]{2,0,1:T(8,128)S(1)} fusion(f32[1,1,176,128,128]{4,3,2,1,0:T(8,128)} %param.10, f32[176,96,128]{2,1,0:T(8,128)} %gather_fusion.2, pred[176]{0:T(512)(128)(4,1)S(1)} %compare_and_fusion), kind=kOutput, calls=%fused_computation.38 | convolution fusion | flops 3324051456 | bytes 28836016 | tf_op jit(solution)/shard_map/sij,vsi->vsj/dot_general | solution.py:23
  751.1 9.6 fusion.14
  760.7 2.3 copy.45
  763.0 117.0 %all-reduce.9.cloned.1.call-done = f32[96,4096]{1,0:T(8,128)} async-done(((f32[96,4096]{1,0:T(8,128)}), f32[96,4096]{1,0:T(8,128)}) %all-reduce.9.cloned.1.call-update) | async-done | bytes 1572880 | tf_op jit(solution)/shard_map/psum | solution.py:53
  880.0 81.7 %reduce-scatter.5.cloned.1.call-done = f32[96,256]{1,0:T(8,128)} async-done(((f32[96,4096]{1,0:T(8,128)}), f32[96,256]{1,0:T(8,128)}) %reduce-scatter.5.cloned.1.call-update) | async-done | bytes 98320 | tf_op jit(solution)/shard_map/reduce_scatter | solution.py:54
  (42 shorter events, 13.4 us)
Async XLA Ops:
  8.7 30.7 %all-to-all-start = ((f32[16,96,256]{2,1,0:T(8,128)}), f32[16,96,256]{2,1,0:T(8,128)S(1)}, u32[]{:S(2)}, u32[]{:S(2)}) async-start(f32[16,96,256]{2,1,0:T(8,128)} %stack.4), calls=%async_computation | async-start | bytes 3145728 | tf_op jit(solution)/shard_map/all_to_all | solution.py:39
  15.8 238.6 %all-reduce.13.cloned.1.call-start = ((), (), s32[]{:S(2)}) async-start(), calls=%async_computation.9 | async-start | bytes 6291456 | tf_op jit(solution)/shard_map/psum | solution.py:11
  54.2 27.2 %copy-start.3 = (s32[1,1,176]{2,1,0:T(1,128)S(1)}, s32[1,1,176]{2,1,0:T(1,128)}, u32[]{:S(2)}) copy-start(s32[1,1,176]{2,1,0:T(1,128)} %param.11) | copy-start | bytes 2116
  93.3 311.8 %all-reduce.7.cloned.1.call-start = ((), (), s32[]{:S(2)}) async-start(), calls=%async_computation.5 | async-start | bytes 3145728 | tf_op jit(solution)/shard_map/psum | solution.py:53
  254.4 2.9 copy-start
  257.2 229.8 %reduce-scatter.3.cloned.1.call-start = ((), (), s32[]{:S(2)}) async-start(), calls=%async_computation.4 | async-start | bytes 1671168 | tf_op jit(solution)/shard_map/reduce_scatter | solution.py:54
  261.8 14.5 %copy-start.4 = (s32[1,1,176]{2,1,0:T(1,128)S(1)}, s32[1,1,176]{2,1,0:T(1,128)}, u32[]{:S(2)}) copy-start(s32[1,1,176]{2,1,0:T(1,128)} %param.12) | copy-start | bytes 2116
  276.2 210.7 %copy-start.2 = (f32[96,256]{1,0:T(8,128)S(1)}, f32[96,256]{1,0:T(8,128)}, u32[]{:S(2)}) copy-start(f32[96,256]{1,0:T(8,128)} %param.9) | copy-start | bytes 294916
  288.1 441.2 %all-reduce.11.cloned.1.call-start = ((), (), s32[]{:S(2)}) async-start(), calls=%async_computation.8 | async-start | bytes 6291456 | tf_op jit(solution)/shard_map/psum | solution.py:11
  570.1 309.9 %all-reduce.9.cloned.1.call-start = ((), (), s32[]{:S(2)}) async-start(), calls=%async_computation.7 | async-start | bytes 3145728 | tf_op jit(solution)/shard_map/psum | solution.py:53
  729.3 2.9 copy-start.1
  732.2 229.6 %reduce-scatter.5.cloned.1.call-start = ((), (), s32[]{:S(2)}) async-start(), calls=%async_computation.6 | async-start | bytes 1671168 | tf_op jit(solution)/shard_map/reduce_scatter | solution.py:54
Sparse Core Ops, SparseCore 0:
  93.4 160.9 all-reduce.12
  257.3 147.7 all-reduce.6
  409.3 77.6 reduce-scatter.2
  570.2 159.0 all-reduce.10
  732.3 147.6 all-reduce.8
  884.1 77.6 reduce-scatter.4
